TPU v7x, 32 devices: a whole 2x2x4 slice. The times are simulated.
32 devices in a mesh: alpha: 8 (over y, x, core), beta: 4 (over z).
Axes of the slice: x: 2, y: 2, z: 4, core: 2. Of those that a mesh axis runs over, the one named last changes fastest.
Arguments:
- coefficients: bfloat16 [4096, 4096], P('alpha', 'beta'), may hold values from -6 to 6
- couplings: bfloat16 [8, 256, 256], replicated, may hold values from -0.375 to 0.375
- exc_list: int32 [8, 8, 3], replicated, may hold values from 0 to 15, as said below
- counts: int32 [8, 8], replicated, may hold values from 0 to 1, as said below
- beta_tiles: bfloat16 [4, 1024, 4096], P(None, None, 'beta'), may hold values from -0.09375 to 0.09375
Outputs:
- sigma_vector: float32 [4096, 4096], P('alpha', 'beta')
Inputs may be any that keep to these rules, and one draw needn't show every extreme that they name: `exc_list`: entry [s, p] describes the slot from alpha device s to alpha device p: field 0 is a source block held by device s (from s * 2 to s * 2 + 1), field 1 a target block held by device p (from p * 2 to p * 2 + 1), field 2 a coupling index below 8. `counts`: 1 where a slot is live, 0 where it is empty; in every draw some device p has a live slot from every device s.
All inputs are finite; a program needn't handle non-finite values.
Results may differ from a plain program's by a relative error of at most 0.0029.
Values may be sent and summed in bfloat16 or wider, within the bound.
A program may use at most 192 MiB of HBM per device.

v0:
```python
import jax
import jax.numpy as jnp
from jax import lax
from jax.sharding import PartitionSpec as P

AB = 256
ABLK = 2
STOPS = 4


def shifted(block, axis, distance):
    devices = range(lax.axis_size(axis))
    route = [((i - distance) % len(devices), i) for i in devices]
    return lax.ppermute(block, axis, route)


def per_device(coefficients, couplings, exc_list, counts, beta_tiles):
    own_index = lax.axis_index("alpha")
    columns = coefficients.shape[1]
    blocks = coefficients.reshape(ABLK, AB, columns)
    incoming = exc_list[:, own_index, :]
    incoming_live = counts[:, own_index] == 1
    block_range = jnp.arange(ABLK, dtype=jnp.int32)
    source_local = jnp.clip(exc_list[own_index, :, 0] - own_index * ABLK, 0, ABLK - 1)
    outgoing = blocks[source_local]
    scaled = couplings[incoming[:, 2]] * incoming_live.astype(jnp.bfloat16)[:, None, None]
    partial_value = jnp.einsum(
        "sij,sjc->sic",
        scaled,
        lax.all_to_all(outgoing, "alpha", split_axis=0, concat_axis=0, tiled=True),
        preferred_element_type=jnp.float32,
    )
    selector = (
        (incoming[:, 1][None, :] - own_index * ABLK == block_range[:, None])
        & incoming_live[None, :]
    ).astype(jnp.float32)
    interm = jnp.einsum("ts,sic->tic", selector, partial_value, precision=lax.Precision.HIGHEST)
    local_rows = interm.astype(jnp.bfloat16).reshape(ABLK * AB, columns)
    summed_out = jnp.dot(local_rows, beta_tiles[0], preferred_element_type=jnp.float32)
    moving = local_rows
    for offset in range(1, STOPS):
        moving = shifted(moving, "beta", 1)
        summed_out = summed_out + jnp.dot(
            moving, beta_tiles[offset], preferred_element_type=jnp.float32
        )
    return summed_out


def solution(mesh):
    placed = (P("alpha", "beta"), P(), P(), P(), P(None, None, "beta"))
    return jax.shard_map(
        per_device, mesh=mesh, in_specs=placed, out_specs=P("alpha", "beta"), check_vma=False
    )
```

profile of v0, /device:TPU:2, one launch (start us, length us, event | category | flops | bytes accessed | tf_op | source)
XLA Modules:
  0.0 149.6 jit_solution(12565810636965616039)
XLA Ops:
  0.0 0.0 copy-start
  0.0 0.8 fusion.31
  0.8 0.4 copy-done
  1.2 2.8 %gather_fusion.1 = bf16[8,256,1024]{2,1,0:T(8,128)(2,1)} fusion(bf16[2,256,1024]{2,1,0:T(8,128)(2,1)S(1)} %bitcast.32, s32[1024]{0:T(1024)S(1)} %pad_clamp_fusion), kind=kCustom, calls=%fused_computation.1 | custom fusion | bytes 8388640 | tf_op jit(solution)/shard_map/gather | solution.py:25
  4.0 0.0 copy-start.3
  4.0 0.0 copy-start.2
  4.0 0.0 copy-start.1
  4.0 4.6 %all-to-all-start = ((bf16[8,256,1024]{2,1,0:T(8,128)(2,1)}), bf16[8,256,1024]{2,1,0:T(8,128)(2,1)}, u32[]{:S(2)}, u32[]{:S(2)}) async-start(bf16[8,256,1024]{2,1,0:T(8,128)(2,1)} %gather_fusion.1), calls=%async_computation | async-start | bytes 8388608 | tf_op jit(solution)/shard_map/all_to_all | solution.py:30
  8.7 0.0 copy-done.3
  8.7 0.2 fusion.22
  8.9 0.0 copy-done.2
  8.9 0.2 dynamic-slice_reduce_fusion
  9.2 0.0 copy-done.1
  9.2 0.6 gather_fusion
  9.8 46.3 %all-to-all-done = bf16[8,256,1024]{2,1,0:T(8,128)(2,1)} async-done(((bf16[8,256,1024]{2,1,0:T(8,128)(2,1)}), bf16[8,256,1024]{2,1,0:T(8,128)(2,1)}, u32[]{:S(2)}, u32[]{:S(2)}) %all-to-all-start) | async-done | bytes 4194336 | tf_op jit(solution)/shard_map/all_to_all | solution.py:30
  56.1 3.5 %fusion.19 = f32[8,256,1024]{2,1,0:T(8,128)S(1)} fusion(bf16[8,256,1024]{2,1,0:T(8,128)(2,1)} %all-to-all-done, bf16[8,256,256]{2,1,0:T(8,128)(2,1)S(1)} %gather_fusion, bf16[8]{0:T(256)(128)(2,1)S(1)} %convert_element_type.11), kind=kOutput, calls=%fused_computation.18 | convolution fusion | flops 1074266112 | bytes 13631504 | tf_op jit(solution)/shard_map/sij,sjc->sic/dot_general | solution.py:27
  59.6 0.0 slice-start
  59.6 0.0 slice-start.1
  59.6 7.4 %fusion.16 = bf16[2,256,1024]{2,0,1:T(2,128)(2,1)S(1)} fusion(f32[8,256,1024]{2,1,0:T(8,128)S(1)} %fusion.19, pred[8]{0:T(512)(128)(4,1)S(1)} %fusion.22, s32[8]{0:T(128)S(1)} %get-tuple-element.5), kind=kOutput, calls=%fused_computation.17 | convolution fusion | flops 50855968 | bytes 9437224 | tf_op jit(solution)/shard_map/ts,sic->tic/dot_general | solution.py:37
  67.0 0.3 copy.6
  67.3 2.4 %collective-permute-start = (bf16[512,1024]{1,0:T(8,128)(2,1)S(1)}, bf16[512,1024]{1,0:T(8,128)(2,1)S(1)}, u32[]{:S(2)}, u32[]{:S(2)}) collective-permute-start(bf16[512,1024]{1,0:T(8,128)(2,1)S(1)} %bitcast.33), channel_id=1, source_target_pairs={{3,0},{0,1},{1,2},{2,3},{7,4},{4,5},{5,6},{6,7},{11,8},{8,9},{9,10... | collective-permute-start | bytes 3145736 | tf_op jit(solution)/shard_map/ppermute | solution.py:14
  69.7 25.4 %collective-permute-done = bf16[512,1024]{1,0:T(8,128)(2,1)S(1)} collective-permute-done((bf16[512,1024]{1,0:T(8,128)(2,1)S(1)}, bf16[512,1024]{1,0:T(8,128)(2,1)S(1)}, u32[]{:S(2)}, u32[]{:S(2)}) %collective-permute-start) | collective-permute-done | bytes 1048608 | tf_op jit(solution)/shard_map/ppermute | solution.py:14
  95.1 0.0 collective-permute-start.1
  95.1 26.3 %collective-permute-done.1 = bf16[512,1024]{1,0:T(8,128)(2,1)S(1)} collective-permute-done((bf16[512,1024]{1,0:T(8,128)(2,1)S(1)}, bf16[512,1024]{1,0:T(8,128)(2,1)S(1)}, u32[]{:S(2)}, u32[]{:S(2)}) %collective-permute-start.1) | collective-permute-done | bytes 1048608 | tf_op jit(solution)/shard_map/ppermute | solution.py:14
  121.4 0.0 collective-permute-start.2
  121.4 2.9 %fusion.8 = f32[512,1024]{1,0:T(8,128)S(1)} fusion(bf16[512,1024]{1,0:T(8,128)(2,1)S(1)} %bitcast.34, bf16[4,1024,1024]{2,1,0:T(8,128)(2,1)} %param.9), kind=kOutput, calls=%fused_computation.10 | convolution fusion | flops 1073741824 | bytes 5242880 | tf_op jit(solution)/shard_map/dot_general | solution.py:39
  124.3 0.0 slice-done
  124.3 0.0 slice-done.1
  124.3 1.3 fusion.6
  125.6 1.3 fusion.4
  126.9 20.1 %collective-permute-done.2 = bf16[512,1024]{1,0:T(8,128)(2,1)S(1)} collective-permute-done((bf16[512,1024]{1,0:T(8,128)(2,1)S(1)}, bf16[512,1024]{1,0:T(8,128)(2,1)S(1)}, u32[]{:S(2)}, u32[]{:S(2)}) %collective-permute-start.2) | collective-permute-done | bytes 1048608 | tf_op jit(solution)/shard_map/ppermute | solution.py:14
  146.9 2.6 %add_add_fusion = f32[512,1024]{1,0:T(8,128)} fusion(f32[512,1024]{1,0:T(8,128)S(1)} %fusion.4, f32[512,1024]{1,0:T(8,128)S(1)} %fusion.8, f32[512,1024]{1,0:T(8,128)S(1)} %fusion.6, bf16[512,1024]{1,0:T(8,128)(2,1)S(1)} %collective-permute-done.2, bf16[4,1024,1024]{2,1,0:T(8,128)(2,1)S(1)} %bitcast.36), kind=kOutput, calls=%fused_computation.13 | convolution fusion | flops 1075314688 | bytes 11534336 | tf_op jit(solution)/shard_map/dot_general | solution.py:43
  (5 shorter events, 0.0 us)
Async XLA Ops:
  0.0 1.2 copy-start
  4.0 4.7 %copy-start.3 = (s32[8,8]{1,0:T(8,128)S(1)}, s32[8,8]{1,0:T(8,128)}, u32[]{:S(2)}) copy-start(s32[8,8]{1,0:T(8,128)} %param.8) | copy-start | bytes 772
  4.0 4.9 %copy-start.2 = (s32[8,8,3]{1,0,2:T(8,128)S(1)}, s32[8,8,3]{1,0,2:T(8,128)}, u32[]{:S(2)}) copy-start(s32[8,8,3]{1,0,2:T(8,128)} %param.7) | copy-start | bytes 2308
  4.0 5.1 %copy-start.1 = (bf16[8,256,256]{2,1,0:T(8,128)(2,1)S(1)}, bf16[8,256,256]{2,1,0:T(8,128)(2,1)}, u32[]{:S(2)}) copy-start(bf16[8,256,256]{2,1,0:T(8,128)(2,1)} %param.6) | copy-start | bytes 3145732
  4.0 52.1 %all-to-all-start = ((bf16[8,256,1024]{2,1,0:T(8,128)(2,1)}), bf16[8,256,1024]{2,1,0:T(8,128)(2,1)}, u32[]{:S(2)}, u32[]{:S(2)}) async-start(bf16[8,256,1024]{2,1,0:T(8,128)(2,1)} %gather_fusion.1), calls=%async_computation | async-start | bytes 8388608 | tf_op jit(solution)/shard_map/all_to_all | solution.py:30
  59.6 64.7 %slice-start = ((s8[8388608]{0:T(1024)(128)(4,1)}), s8[4194304]{0:T(1024)(128)(4,1)S(1)}, s32[]{:S(2)}) async-start(s8[8388608]{0:T(1024)(128)(4,1)} %bitcast.35), calls=%async_computation.1 | async-start | bytes 8388608
  59.6 64.7 %slice-start.1 = ((s8[8388608]{0:T(1024)(128)(4,1)}), s8[4194304]{0:T(1024)(128)(4,1)S(1)}, s32[]{:S(2)}) async-start(s8[8388608]{0:T(1024)(128)(4,1)} %bitcast.35), calls=%async_computation.2 | async-start | bytes 8388608
  67.3 27.8 %collective-permute-start = (bf16[512,1024]{1,0:T(8,128)(2,1)S(1)}, bf16[512,1024]{1,0:T(8,128)(2,1)S(1)}, u32[]{:S(2)}, u32[]{:S(2)}) collective-permute-start(bf16[512,1024]{1,0:T(8,128)(2,1)S(1)} %bitcast.33), channel_id=1, source_target_pairs={{3,0},{0,1},{1,2},{2,3},{7,4},{4,5},{5,6},{6,7},{11,8},{8,9},{9,10... | collective-permute-start | bytes 3145736 | tf_op jit(solution)/shard_map/ppermute | solution.py:14
  95.1 26.3 %collective-permute-start.1 = (bf16[512,1024]{1,0:T(8,128)(2,1)S(1)}, bf16[512,1024]{1,0:T(8,128)(2,1)S(1)}, u32[]{:S(2)}, u32[]{:S(2)}) collective-permute-start(bf16[512,1024]{1,0:T(8,128)(2,1)S(1)} %collective-permute-done), channel_id=1, source_target_pairs={{3,0},{0,1},{1,2},{2,3},{7,4},{4,5},{5,6},{6,7},{11,8},{8,9},{9,10... | collective-permute-start | bytes 3145736 | tf_op jit(solution)/shard_map/ppermute | solution.py:14
  121.4 25.5 %collective-permute-start.2 = (bf16[512,1024]{1,0:T(8,128)(2,1)S(1)}, bf16[512,1024]{1,0:T(8,128)(2,1)S(1)}, u32[]{:S(2)}, u32[]{:S(2)}) collective-permute-start(bf16[512,1024]{1,0:T(8,128)(2,1)S(1)} %collective-permute-done.1), channel_id=1, source_target_pairs={{3,0},{0,1},{1,2},{2,3},{7,4},{4,5},{5,6},{6,7},{11,8},{8,9},{9,10... | collective-permute-start | bytes 3145736 | tf_op jit(solution)/shard_map/ppermute | solution.py:14
where the time goes:
time: 150 us
  waiting for transfers between devices  118 us (79%)
  matrix products  18.9 us (13%)
  starting transfers between devices  7.02 us (5%)
  local copies, waits for them, and re-layouts  4.36 us (3%)
    ppermute x3, waiting for transfers between devices, shifted(): return lax.ppermute(block, axis, route)  71.8 us
    all_to_all x1, waiting for transfers between devices, per_device(): lax.all_to_all(outgoing, 'alpha', split_axis=0, concat_axis=0, tiled=True)  46.3 us
    dot_general x1, matrix products, per_device(): jnp.einsum('ts,sic->tic', selector, partial_value, precision=lax.Precisio...  7.42 us
    dot_general x3, matrix products, per_device(): jnp.dot(moving, beta_tiles[offset], preferred_element_type=jnp.float32)  5.16 us
    all_to_all x1, starting transfers between devices, per_device(): lax.all_to_all(outgoing, 'alpha', split_axis=0, concat_axis=0, tiled=True)  4.65 us
    dot_general x1, matrix products, per_device(): jnp.einsum('sij,sjc->sic', scaled, lax.all_to_all(outgoing, 'alpha', spli...  3.48 us
  transfers between devices with their start and end apart: 4, of which 4 were waited for; matrix products, arithmetic and copies ran while one was open for 4% of the time, Pallas kernels for 0%

commit v1 on v0

v1 whole, which is shorter than its diff:
```python
import functools

import jax
import jax.numpy as jnp
from jax import lax
from jax.experimental import pallas as pl
from jax.experimental.pallas import tpu as pltpu
from jax.sharding import PartitionSpec as P

MESH = pl.DeviceIdType.MESH
CHUNK = 256
TILE = 256
AHEAD = 2


def flip(position, mask):
    bit = lax.rem(lax.div(position, mask), 2)
    return position + mask * (1 - 2 * bit)


def kernel(
    n_alpha, n_beta, rounds, chunks,
    exc_ref, counts_ref, coupling_ref, c_hbm, b_hbm, out_ref,
    weights, gathered, tiles, held, moved,
    send_sem, recv_sem, own_sem, zsend_sem, zrecv_sem, tile_sem,
):
    n_chips = n_alpha // 2
    n_blocks, order = c_hbm.shape[0], c_hbm.shape[1]
    n_stops = b_hbm.shape[0]
    width = CHUNK
    alpha, beta = lax.axis_index("alpha"), lax.axis_index("beta")
    chip, core = lax.div(alpha, 2), lax.rem(alpha, 2)

    def mask_of(step, which):
        return (1 - which) * 2**step + which * 2 ** (rounds - 1 - step)

    def origin(label, which):
        source = chip
        for step in range(rounds):
            if (label >> step) & 1:
                source = flip(source, mask_of(step, which))
        return source * 2 + which

    if n_beta == n_stops:
        way, far, near = 1 - 2 * core, n_beta // 2, n_beta - 1 - n_beta // 2
    else:
        way, far, near = 1, n_stops - 1, 0
    ahead = lax.rem(beta + way + n_beta, n_beta)
    behind = lax.rem(beta - way + n_beta, n_beta)

    sibling = (alpha + 1 - 2 * core, beta)
    neighbours = [(flip(chip, mask_of(step, core)) * 2 + core, beta) for step in range(rounds)]
    greeted = neighbours + [sibling, (alpha, ahead), (alpha, behind)]
    barrier = pltpu.get_barrier_semaphore()
    for device in greeted:
        pl.semaphore_signal(barrier, inc=1, device_id=device, device_id_type=MESH)
    own = []
    for c in range(chunks):
        own.append(
            pltpu.make_async_copy(c_hbm.at[:, :, pl.ds(c * width, width)], held[c].at[0], own_sem.at[c])
        )
    own[0].start()
    pl.semaphore_wait(barrier, len(greeted))

    def to_alpha(c, label, target, device):
        source = c_hbm.at[:, :, pl.ds(c * width, width)] if label == 0 else held[c].at[label]
        return pltpu.make_async_remote_copy(
            src_ref=source,
            dst_ref=held[c].at[target],
            send_sem=send_sem.at[c, target],
            recv_sem=recv_sem.at[c, target],
            device_id=device,
            device_id_type=MESH,
        )

    copies = [{} for _ in range(chunks)]

    def pass_on(c, label):
        for step in range(label.bit_length(), rounds):
            target = label + 2**step
            copies[c][target] = to_alpha(c, label, target, neighbours[step])
            copies[c][target].start()
        target = n_chips + label
        copies[c][target] = to_alpha(c, label, target, sibling)
        copies[c][target].start()

    def slot_of(hop):
        return lax.rem(hop * way + n_beta * n_stops, n_beta)

    hops = [{} for _ in range(chunks)]

    def to_beta(c, kind, hop):
        sign, device, index = (1, ahead, hop - 1) if kind == "far" else (-1, behind, far + hop - 1)
        copy = pltpu.make_async_remote_copy(
            src_ref=moved[c].at[slot_of(sign * (hop - 1))],
            dst_ref=moved[c].at[slot_of(sign * hop)],
            send_sem=zsend_sem.at[c, index],
            recv_sem=zrecv_sem.at[c, index],
            device_id=(alpha, device),
            device_id_type=MESH,
        )
        hops[c][kind, hop] = copy
        copy.start()

    for c in range(min(AHEAD, chunks)):
        if c > 0:
            own[c].start()
        pass_on(c, 0)
    tile_copy = pltpu.make_async_copy(b_hbm, tiles, tile_sem)
    tile_copy.start()

    sources = [origin(label, core) for label in range(n_chips)]
    sources += [origin(label, 1 - core) for label in range(n_chips)]
    picked = []
    for slot, source in enumerate(sources):
        entry = (source * n_alpha + alpha) * 3
        live = counts_ref[source * n_alpha + alpha] == 1
        picked.append(jnp.clip(exc_ref[entry] - source * n_blocks, 0, n_blocks - 1))
        target = exc_ref[entry + 1] - alpha * n_blocks
        matrix = coupling_ref[exc_ref[entry + 2]]
        for block in range(n_blocks):
            keep = jnp.where(live & (target == block), 1.0, 0.0).astype(jnp.float32)
            weights[pl.ds(block * order, order), pl.ds(slot * order, order)] = (
                matrix.astype(jnp.float32) * keep
            ).astype(jnp.bfloat16)

    def product(c):
        @pl.loop(0, out_ref.shape[1] // TILE)
        def _(n):
            columns = pl.ds(pl.multiple_of(n * TILE, TILE), TILE)
            left = jnp.concatenate([moved[c][d] for d in range(n_stops)], axis=1)
            right = jnp.concatenate(
                [tiles[d, pl.ds(c * width, width), columns] for d in range(n_stops)], axis=0
            )
            value = jnp.dot(left, right, preferred_element_type=jnp.float32)
            if c == 0:
                out_ref[:, columns] = value
            else:
                out_ref[:, columns] += value

    def relay(c):
        for kind, last in (("far", far), ("near", near)):
            for hop in range(1, last):
                hops[c][kind, hop].wait_recv()
                to_beta(c, kind, hop + 1)

    def finish(c):
        for kind, last in (("far", far), ("near", near)):
            if last > 0:
                hops[c][kind, last].wait_recv()
        if c == 0:
            tile_copy.wait()
        product(c)

    for c in range(chunks):
        for label in range(1, n_chips):
            copies[c][label].wait_recv()
            pass_on(c, label)
            if label == 1 and c + AHEAD < chunks:
                own[c + AHEAD].start()
                pass_on(c + AHEAD, 0)
        own[c].wait()
        for label in range(n_chips):
            copies[c][n_chips + label].wait_recv()
        for slot in range(n_alpha):
            gathered[pl.ds(slot * order, order), :] = held[c][slot, picked[slot]]
        moved[c][0] = jnp.dot(
            weights[...], gathered[...], preferred_element_type=jnp.float32
        ).astype(jnp.bfloat16)
        to_beta(c, "far", 1)
        if near > 0:
            to_beta(c, "near", 1)
        if c >= 1:
            relay(c - 1)
        if c >= 2:
            finish(c - 2)
    relay(chunks - 1)
    for c in range(max(chunks - 2, 0), chunks):
        finish(c)
    for c in range(chunks):
        for copy in copies[c].values():
            copy.wait_send()
        for copy in hops[c].values():
            copy.wait_send()


def solution(mesh):
    n_alpha, n_beta = mesh.shape["alpha"], mesh.shape["beta"]
    n_chips = n_alpha // 2
    rounds = n_chips.bit_length() - 1

    def per_device(coefficients, couplings, exc_list, counts, beta_tiles):
        order = couplings.shape[1]
        rows, columns = coefficients.shape
        n_blocks = rows // order
        n_stops = beta_tiles.shape[0]
        chunks = columns // CHUNK
        vmem, smem = pl.BlockSpec(memory_space=pltpu.VMEM), pl.BlockSpec(memory_space=pltpu.SMEM)
        hbm = pl.BlockSpec(memory_space=pl.ANY)
        return pl.pallas_call(
            functools.partial(kernel, n_alpha, n_beta, rounds, chunks),
            out_shape=jax.ShapeDtypeStruct((rows, columns), jnp.float32),
            in_specs=[smem, smem, vmem, hbm, hbm],
            out_specs=vmem,
            scratch_shapes=[
                pltpu.VMEM((rows, n_alpha * order), jnp.bfloat16),
                pltpu.VMEM((n_alpha * order, CHUNK), jnp.bfloat16),
                pltpu.VMEM(beta_tiles.shape, jnp.bfloat16),
                [pltpu.VMEM((n_alpha, n_blocks, order, CHUNK), jnp.bfloat16) for _ in range(chunks)],
                [pltpu.VMEM((n_stops, rows, CHUNK), jnp.bfloat16) for _ in range(chunks)],
                pltpu.SemaphoreType.DMA((chunks, n_alpha)),
                pltpu.SemaphoreType.DMA((chunks, n_alpha)),
                pltpu.SemaphoreType.DMA((chunks,)),
                pltpu.SemaphoreType.DMA((chunks, n_stops - 1)),
                pltpu.SemaphoreType.DMA((chunks, n_stops - 1)),
                pltpu.SemaphoreType.DMA(()),
            ],
            compiler_params=pltpu.CompilerParams(
                collective_id=0, has_side_effects=True, vmem_limit_bytes=60 * 2**20
            ),
        )(
            exc_list.reshape(-1),
            counts.reshape(-1),
            couplings,
            coefficients.reshape(n_blocks, order, columns),
            beta_tiles,
        )

    placed = (P("alpha", "beta"), P(), P(), P(), P(None, None, "beta"))
    return jax.shard_map(
        per_device, mesh=mesh, in_specs=placed, out_specs=P("alpha", "beta"), check_vma=False
    )
```

time: 150 us -> 107 us (0.71)
  the two profiles are of different devices: /device:TPU:2 before, /device:TPU:0 now
where the time goes in v1:
time: 107 us; the launch traced here: 106 us
  Pallas kernels  100 us (93%)
  local copies, waits for them, and re-layouts  5.97 us (6%)
    pallas_call x1, Pallas kernels, per_device(): pl.pallas_call(functools.partial(kernel, n_alpha, n_beta, rounds, chunks)...  100 us
    unnamed x2, local copies, waits for them, and re-layouts  3.98 us

profile of v1, /device:TPU:0, one launch (start us, length us, event | category | flops | bytes accessed | tf_op | source)
XLA Modules:
  0.0 106.3 jit_solution(5666856584454736614)
XLA Ops:
  0.0 1.3 %reshape.10.counts_ref = s32[64]{0:T(128)} reshape(s32[8,8]{1,0:T(8,128)} %param.8) | data formatting | bytes 512 | tf_op jit(solution)/shard_map/reshape | solution.py:223
  1.3 0.8 copy.6
  2.1 0.7 reshape.9.exc_ref
  2.8 100.3 %shard_map.55 = f32[512,1024]{1,0:T(8,128)} custom-call(s32[192]{0:T(256)} %reshape.9.exc_ref, s32[64]{0:T(128)} %reshape.10.counts_ref, bf16[8,256,256]{2,1,0:T(8,128)(2,1)} %coupling_ref.1, bf16[2,256,1024]{2,1,0:T(8,128)(2,1)} %bitcast.1, bf16[4,1024,1024]{2,1,0:T(8,128)(2,1)} %b_hbm.1), custom_call_target="tpu_custom_call" | custom-call | tf_op jit(solution)/shard_map/pallas_call | solution.py:200
  103.1 3.2 %copy.8 = f32[512,1024]{1,0:T(8,128)} copy(f32[512,1024]{1,0:T(8,128)} %shard_map.55) | data formatting | bytes 4194304

commit v2 on v1

--- a/solution.py
+++ b/solution.py
@@ -8,9 +8,9 @@
 from jax.sharding import PartitionSpec as P
 
 MESH = pl.DeviceIdType.MESH
-CHUNK = 256
+CHUNK = 128
 TILE = 256
-AHEAD = 2
+AHEAD = 1
 
 
 def flip(position, mask):
@@ -41,12 +41,8 @@
                 source = flip(source, mask_of(step, which))
         return source * 2 + which
 
-    if n_beta == n_stops:
-        way, far, near = 1 - 2 * core, n_beta // 2, n_beta - 1 - n_beta // 2
-    else:
-        way, far, near = 1, n_stops - 1, 0
-    ahead = lax.rem(beta + way + n_beta, n_beta)
-    behind = lax.rem(beta - way + n_beta, n_beta)
+    line = n_beta == n_stops
+    ahead, behind = lax.rem(beta + 1, n_beta), lax.rem(beta + n_beta - 1, n_beta)
 
     sibling = (alpha + 1 - 2 * core, beta)
     neighbours = [(flip(chip, mask_of(step, core)) * 2 + core, beta) for step in range(rounds)]
@@ -84,23 +80,34 @@
         copies[c][target] = to_alpha(c, label, target, sibling)
         copies[c][target].start()
 
-    def slot_of(hop):
-        return lax.rem(hop * way + n_beta * n_stops, n_beta)
-
-    hops = [{} for _ in range(chunks)]
-
-    def to_beta(c, kind, hop):
-        sign, device, index = (1, ahead, hop - 1) if kind == "far" else (-1, behind, far + hop - 1)
-        copy = pltpu.make_async_remote_copy(
-            src_ref=moved[c].at[slot_of(sign * (hop - 1))],
-            dst_ref=moved[c].at[slot_of(sign * hop)],
-            send_sem=zsend_sem.at[c, index],
-            recv_sem=zrecv_sem.at[c, index],
-            device_id=(alpha, device),
+    def to_beta(c, sign, hop):
+        source, target = sign * (hop - 1) % n_stops, sign * hop % n_stops
+        return pltpu.make_async_remote_copy(
+            src_ref=moved[c].at[source],
+            dst_ref=moved[c].at[target],
+            send_sem=zsend_sem.at[c, hop - 1 if sign == 1 else n_stops + hop - 2],
+            recv_sem=zrecv_sem.at[c, target - 1],
+            device_id=(alpha, ahead if sign == 1 else behind),
             device_id_type=MESH,
         )
-        hops[c][kind, hop] = copy
-        copy.start()
+
+    def sends(sign, hop):
+        if not line:
+            return sign == 1
+        if sign == 1:
+            return (beta >= hop - 1) & (beta <= n_beta - 2)
+        return (beta <= n_beta - hop) & (beta >= 1)
+
+    def send_beta(c, sign, hop):
+        if 1 <= hop < n_stops and (line or sign == 1):
+            pl.when(sends(sign, hop))(lambda: to_beta(c, sign, hop).start())
+
+    def relay(c, slots):
+        for slot in slots:
+            to_beta(c, 1, slot).wait_recv()
+            send_beta(c, 1, slot + 1)
+            if line:
+                send_beta(c, -1, n_stops - slot + 1)
 
     for c in range(min(AHEAD, chunks)):
         if c > 0:
@@ -113,11 +120,10 @@
     sources += [origin(label, 1 - core) for label in range(n_chips)]
     picked = []
     for slot, source in enumerate(sources):
-        entry = (source * n_alpha + alpha) * 3
-        live = counts_ref[source * n_alpha + alpha] == 1
-        picked.append(jnp.clip(exc_ref[entry] - source * n_blocks, 0, n_blocks - 1))
-        target = exc_ref[entry + 1] - alpha * n_blocks
-        matrix = coupling_ref[exc_ref[entry + 2]]
+        live = counts_ref[source, alpha] == 1
+        picked.append(jnp.clip(exc_ref[0, source, alpha] - source * n_blocks, 0, n_blocks - 1))
+        target = exc_ref[1, source, alpha] - alpha * n_blocks
+        matrix = coupling_ref[exc_ref[2, source, alpha]]
         for block in range(n_blocks):
             keep = jnp.where(live & (target == block), 1.0, 0.0).astype(jnp.float32)
             weights[pl.ds(block * order, order), pl.ds(slot * order, order)] = (
@@ -138,19 +144,17 @@
             else:
                 out_ref[:, columns] += value
 
-    def relay(c):
-        for kind, last in (("far", far), ("near", near)):
-            for hop in range(1, last):
-                hops[c][kind, hop].wait_recv()
-                to_beta(c, kind, hop + 1)
-
-    def finish(c):
-        for kind, last in (("far", far), ("near", near)):
-            if last > 0:
-                hops[c][kind, last].wait_recv()
-        if c == 0:
-            tile_copy.wait()
-        product(c)
+    near = (1, n_stops - 1) if line else (1,)
+    later = [slot for slot in range(1, n_stops) if slot not in near]
+
+    def behind_by(c):
+        if 0 <= c - 1 < chunks:
+            relay(c - 1, near)
+        if 0 <= c - 2 < chunks:
+            relay(c - 2, later)
+            if c == 2:
+                tile_copy.wait()
+            product(c - 2)
 
     for c in range(chunks):
         for label in range(1, n_chips):
@@ -167,21 +171,18 @@
         moved[c][0] = jnp.dot(
             weights[...], gathered[...], preferred_element_type=jnp.float32
         ).astype(jnp.bfloat16)
-        to_beta(c, "far", 1)
-        if near > 0:
-            to_beta(c, "near", 1)
-        if c >= 1:
-            relay(c - 1)
-        if c >= 2:
-            finish(c - 2)
-    relay(chunks - 1)
-    for c in range(max(chunks - 2, 0), chunks):
-        finish(c)
+        send_beta(c, 1, 1)
+        send_beta(c, -1, 1)
+        behind_by(c)
+    behind_by(chunks)
+    behind_by(chunks + 1)
     for c in range(chunks):
         for copy in copies[c].values():
             copy.wait_send()
-        for copy in hops[c].values():
-            copy.wait_send()
+        for sign in (1, -1):
+            for hop in range(1, n_stops):
+                if line or sign == 1:
+                    pl.when(sends(sign, hop))(lambda: to_beta(c, sign, hop).wait_send())
 
 
 def solution(mesh):
@@ -199,7 +200,7 @@
         hbm = pl.BlockSpec(memory_space=pl.ANY)
         return pl.pallas_call(
             functools.partial(kernel, n_alpha, n_beta, rounds, chunks),
-            out_shape=jax.ShapeDtypeStruct((rows, columns), jnp.float32),
+            out_shape=pltpu.VMEM((rows, columns), jnp.float32),
             in_specs=[smem, smem, vmem, hbm, hbm],
             out_specs=vmem,
             scratch_shapes=[
@@ -211,16 +212,16 @@
                 pltpu.SemaphoreType.DMA((chunks, n_alpha)),
                 pltpu.SemaphoreType.DMA((chunks, n_alpha)),
                 pltpu.SemaphoreType.DMA((chunks,)),
-                pltpu.SemaphoreType.DMA((chunks, n_stops - 1)),
+                pltpu.SemaphoreType.DMA((chunks, 2 * n_stops - 2)),
                 pltpu.SemaphoreType.DMA((chunks, n_stops - 1)),
                 pltpu.SemaphoreType.DMA(()),
             ],
             compiler_params=pltpu.CompilerParams(
-                collective_id=0, has_side_effects=True, vmem_limit_bytes=60 * 2**20
+                collective_id=0, has_side_effects=True, vmem_limit_bytes=48 * 2**20
             ),
         )(
-            exc_list.reshape(-1),
-            counts.reshape(-1),
+            exc_list.transpose(2, 0, 1),
+            counts,
             couplings,
             coefficients.reshape(n_blocks, order, columns),
             beta_tiles,

time: 107 us -> 165 us (1.54)
  Pallas kernels: 100 us -> 159 us
    pallas_call x1, Pallas kernels: 100 us -> 159 us  [per_device(): pl.pallas_call(functools.partial(kernel, n_alpha, n_beta, rounds, chunks)...]
    reshape x2 -> x0, local copies, waits for them, and re-layouts: 1.99 us -> none  [the longest x1 1.28 us: per_device(): counts.reshape(-1)]
    unnamed x2 -> x9, local copies, waits for them, and re-layouts: 3.98 us -> 5.16 us
where the time goes in v2:
time: 165 us; the launch traced here: 164 us
  Pallas kernels  159 us (96%)
  local copies, waits for them, and re-layouts  5.16 us (3%)
    pallas_call x1, Pallas kernels, per_device(): pl.pallas_call(functools.partial(kernel, n_alpha, n_beta, rounds, chunks)...  159 us
    unnamed x9, local copies, waits for them, and re-layouts  5.16 us

profile of v2, /device:TPU:0, one launch (start us, length us, event | category | flops | bytes accessed | tf_op | source)
XLA Modules:
  0.0 164.1 jit_solution(16972563485733557921)
XLA Ops:
  0.0 0.0 copy-start
  0.0 1.2 copy-done
  1.2 0.0 copy-start.1
  1.2 1.2 copy-done.1
  2.5 0.0 copy-start.2
  2.5 0.7 copy-done.2
  3.2 0.0 copy-start.3
  3.2 0.7 copy-done.3
  3.8 158.9 %shard_map.55 = f32[512,1024]{1,0:T(8,128)S(1)} custom-call(s32[3,8,8]{2,1,0:T(8,128)S(1)} %bitcast.3, s32[8,8]{1,0:T(8,128)S(1)} %copy-done.3, bf16[8,256,256]{2,1,0:T(8,128)(2,1)S(1)} %copy-done, bf16[2,256,1024]{2,1,0:T(8,128)(2,1)S(1)} %bitcast.2, bf16[4,1024,1024]{2,1,0:T(8,128)(2,1)} %b_hbm.1), custom_call_target="tpu_custom_call" | custom-call | tf_op jit(solution)/shard_map/pallas_call | solution.py:201
  162.8 1.3 copy.7
Async XLA Ops:
  0.0 1.2 copy-start
  1.2 1.2 copy-start.1
  2.5 0.7 copy-start.2
  3.2 0.7 copy-start.3

commit v3 on v1

--- a/solution.py
+++ b/solution.py
@@ -10,7 +10,7 @@
 MESH = pl.DeviceIdType.MESH
 CHUNK = 256
 TILE = 256
-AHEAD = 2
+AHEAD = 1
 
 
 def flip(position, mask):
@@ -113,11 +113,10 @@
     sources += [origin(label, 1 - core) for label in range(n_chips)]
     picked = []
     for slot, source in enumerate(sources):
-        entry = (source * n_alpha + alpha) * 3
-        live = counts_ref[source * n_alpha + alpha] == 1
-        picked.append(jnp.clip(exc_ref[entry] - source * n_blocks, 0, n_blocks - 1))
-        target = exc_ref[entry + 1] - alpha * n_blocks
-        matrix = coupling_ref[exc_ref[entry + 2]]
+        live = counts_ref[source, alpha] == 1
+        picked.append(jnp.clip(exc_ref[0, source, alpha] - source * n_blocks, 0, n_blocks - 1))
+        target = exc_ref[1, source, alpha] - alpha * n_blocks
+        matrix = coupling_ref[exc_ref[2, source, alpha]]
         for block in range(n_blocks):
             keep = jnp.where(live & (target == block), 1.0, 0.0).astype(jnp.float32)
             weights[pl.ds(block * order, order), pl.ds(slot * order, order)] = (
@@ -199,7 +198,7 @@
         hbm = pl.BlockSpec(memory_space=pl.ANY)
         return pl.pallas_call(
             functools.partial(kernel, n_alpha, n_beta, rounds, chunks),
-            out_shape=jax.ShapeDtypeStruct((rows, columns), jnp.float32),
+            out_shape=pltpu.VMEM((rows, columns), jnp.float32),
             in_specs=[smem, smem, vmem, hbm, hbm],
             out_specs=vmem,
             scratch_shapes=[
@@ -216,11 +215,11 @@
                 pltpu.SemaphoreType.DMA(()),
             ],
             compiler_params=pltpu.CompilerParams(
-                collective_id=0, has_side_effects=True, vmem_limit_bytes=60 * 2**20
+                collective_id=0, has_side_effects=True, vmem_limit_bytes=48 * 2**20
             ),
         )(
-            exc_list.reshape(-1),
-            counts.reshape(-1),
+            exc_list.transpose(2, 0, 1),
+            counts,
             couplings,
             coefficients.reshape(n_blocks, order, columns),
             beta_tiles,

time: 107 us -> 99.6 us (0.931)
  Pallas kernels: 100 us -> 94.2 us
    pallas_call x1, Pallas kernels: 100 us -> 94.2 us  [per_device(): pl.pallas_call(functools.partial(kernel, n_alpha, n_beta, rounds, chunks)...]
    reshape x2 -> x0, local copies, waits for them, and re-layouts: 1.99 us -> none  [the longest x1 1.28 us: per_device(): counts.reshape(-1)]
    unnamed x2 -> x9, local copies, waits for them, and re-layouts: 3.98 us -> 5.16 us
where the time goes in v3:
time: 99.6 us; the launch traced here: 99.4 us
  Pallas kernels  94.2 us (95%)
  local copies, waits for them, and re-layouts  5.16 us (5%)
    pallas_call x1, Pallas kernels, per_device(): pl.pallas_call(functools.partial(kernel, n_alpha, n_beta, rounds, chunks)...  94.2 us
    unnamed x9, local copies, waits for them, and re-layouts  5.16 us

profile of v3, /device:TPU:0, one launch (start us, length us, event | category | flops | bytes accessed | tf_op | source)
XLA Modules:
  0.0 99.4 jit_solution(6064254420123210869)
XLA Ops:
  0.0 0.0 copy-start
  0.0 1.2 %copy-done = bf16[8,256,256]{2,1,0:T(8,128)(2,1)S(1)} copy-done((bf16[8,256,256]{2,1,0:T(8,128)(2,1)S(1)}, bf16[8,256,256]{2,1,0:T(8,128)(2,1)}, u32[]{:S(2)}) %copy-start) | copy-done | bytes 1048600
  1.2 0.0 copy-start.1
  1.2 1.2 %copy-done.1 = bf16[512,1024]{1,0:T(8,128)(2,1)S(1)} copy-done((bf16[512,1024]{1,0:T(8,128)(2,1)S(1)}, bf16[512,1024]{1,0:T(8,128)(2,1)}, u32[]{:S(2)}) %copy-start.1) | copy-done | bytes 1048600
  2.5 0.0 copy-start.2
  2.5 0.7 copy-done.2
  3.2 0.0 copy-start.3
  3.2 0.7 copy-done.3
  3.8 94.2 %shard_map.55 = f32[512,1024]{1,0:T(8,128)S(1)} custom-call(s32[3,8,8]{2,1,0:T(8,128)S(1)} %bitcast.3, s32[8,8]{1,0:T(8,128)S(1)} %copy-done.3, bf16[8,256,256]{2,1,0:T(8,128)(2,1)S(1)} %copy-done, bf16[2,256,1024]{2,1,0:T(8,128)(2,1)S(1)} %bitcast.2, bf16[4,1024,1024]{2,1,0:T(8,128)(2,1)} %b_hbm.1), custom_call_target="tpu_custom_call" | custom-call | tf_op jit(solution)/shard_map/pallas_call | solution.py:199
  98.0 1.3 %copy.7 = f32[512,1024]{1,0:T(8,128)} copy(f32[512,1024]{1,0:T(8,128)S(1)} %shard_map.55) | data formatting | bytes 4194304
Async XLA Ops:
  0.0 1.2 %copy-start = (bf16[8,256,256]{2,1,0:T(8,128)(2,1)S(1)}, bf16[8,256,256]{2,1,0:T(8,128)(2,1)}, u32[]{:S(2)}) copy-start(bf16[8,256,256]{2,1,0:T(8,128)(2,1)} %coupling_ref.1) | copy-start | bytes 3145732
  1.2 1.2 %copy-start.1 = (bf16[512,1024]{1,0:T(8,128)(2,1)S(1)}, bf16[512,1024]{1,0:T(8,128)(2,1)}, u32[]{:S(2)}) copy-start(bf16[512,1024]{1,0:T(8,128)(2,1)} %param.5) | copy-start | bytes 3145732
  2.5 0.7 copy-start.2
  3.2 0.7 copy-start.3

commit v4 on v3

--- a/solution.py
+++ b/solution.py
@@ -8,9 +8,15 @@
 from jax.sharding import PartitionSpec as P
 
 MESH = pl.DeviceIdType.MESH
-CHUNK = 256
+WIDTHS = (1, 2, 2, 2, 1)
 TILE = 256
 AHEAD = 1
+
+
+def split(columns):
+    unit = columns // sum(WIDTHS)
+    widths = [unit * part for part in WIDTHS]
+    return widths, [sum(widths[:c]) for c in range(len(widths))]
 
 
 def flip(position, mask):
@@ -27,7 +33,7 @@
     n_chips = n_alpha // 2
     n_blocks, order = c_hbm.shape[0], c_hbm.shape[1]
     n_stops = b_hbm.shape[0]
-    width = CHUNK
+    widths, starts = split(out_ref.shape[1])
     alpha, beta = lax.axis_index("alpha"), lax.axis_index("beta")
     chip, core = lax.div(alpha, 2), lax.rem(alpha, 2)
 
@@ -57,13 +63,13 @@
     own = []
     for c in range(chunks):
         own.append(
-            pltpu.make_async_copy(c_hbm.at[:, :, pl.ds(c * width, width)], held[c].at[0], own_sem.at[c])
+            pltpu.make_async_copy(c_hbm.at[:, :, pl.ds(starts[c], widths[c])], held[c].at[0], own_sem.at[c])
         )
     own[0].start()
     pl.semaphore_wait(barrier, len(greeted))
 
     def to_alpha(c, label, target, device):
-        source = c_hbm.at[:, :, pl.ds(c * width, width)] if label == 0 else held[c].at[label]
+        source = c_hbm.at[:, :, pl.ds(starts[c], widths[c])] if label == 0 else held[c].at[label]
         return pltpu.make_async_remote_copy(
             src_ref=source,
             dst_ref=held[c].at[target],
@@ -129,7 +135,7 @@
             columns = pl.ds(pl.multiple_of(n * TILE, TILE), TILE)
             left = jnp.concatenate([moved[c][d] for d in range(n_stops)], axis=1)
             right = jnp.concatenate(
-                [tiles[d, pl.ds(c * width, width), columns] for d in range(n_stops)], axis=0
+                [tiles[d, pl.ds(starts[c], widths[c]), columns] for d in range(n_stops)], axis=0
             )
             value = jnp.dot(left, right, preferred_element_type=jnp.float32)
             if c == 0:
@@ -162,9 +168,9 @@
         for label in range(n_chips):
             copies[c][n_chips + label].wait_recv()
         for slot in range(n_alpha):
-            gathered[pl.ds(slot * order, order), :] = held[c][slot, picked[slot]]
+            gathered[pl.ds(slot * order, order), pl.ds(0, widths[c])] = held[c][slot, picked[slot]]
         moved[c][0] = jnp.dot(
-            weights[...], gathered[...], preferred_element_type=jnp.float32
+            weights[...], gathered[:, pl.ds(0, widths[c])], preferred_element_type=jnp.float32
         ).astype(jnp.bfloat16)
         to_beta(c, "far", 1)
         if near > 0:
@@ -193,7 +199,8 @@
         rows, columns = coefficients.shape
         n_blocks = rows // order
         n_stops = beta_tiles.shape[0]
-        chunks = columns // CHUNK
+        widths, _ = split(columns)
+        chunks = len(widths)
         vmem, smem = pl.BlockSpec(memory_space=pltpu.VMEM), pl.BlockSpec(memory_space=pltpu.SMEM)
         hbm = pl.BlockSpec(memory_space=pl.ANY)
         return pl.pallas_call(
@@ -203,10 +210,10 @@
             out_specs=vmem,
             scratch_shapes=[
                 pltpu.VMEM((rows, n_alpha * order), jnp.bfloat16),
-                pltpu.VMEM((n_alpha * order, CHUNK), jnp.bfloat16),
+                pltpu.VMEM((n_alpha * order, max(widths)), jnp.bfloat16),
                 pltpu.VMEM(beta_tiles.shape, jnp.bfloat16),
-                [pltpu.VMEM((n_alpha, n_blocks, order, CHUNK), jnp.bfloat16) for _ in range(chunks)],
-                [pltpu.VMEM((n_stops, rows, CHUNK), jnp.bfloat16) for _ in range(chunks)],
+                [pltpu.VMEM((n_alpha, n_blocks, order, width), jnp.bfloat16) for width in widths],
+                [pltpu.VMEM((n_stops, rows, width), jnp.bfloat16) for width in widths],
                 pltpu.SemaphoreType.DMA((chunks, n_alpha)),
                 pltpu.SemaphoreType.DMA((chunks, n_alpha)),
                 pltpu.SemaphoreType.DMA((chunks,)),

time: 99.6 us -> 98.6 us (0.990)
  Pallas kernels: 94.2 us -> 93.1 us
    pallas_call x1, Pallas kernels: 94.2 us -> 93.1 us  [per_device(): pl.pallas_call(functools.partial(kernel, n_alpha, n_beta, rounds, chunks)...]
where the time goes in v4:
time: 98.6 us; the launch traced here: 98.3 us
  Pallas kernels  93.1 us (94%)
  local copies, waits for them, and re-layouts  5.16 us (5%)
    pallas_call x1, Pallas kernels, per_device(): pl.pallas_call(functools.partial(kernel, n_alpha, n_beta, rounds, chunks)...  93.1 us
    unnamed x9, local copies, waits for them, and re-layouts  5.16 us

profile of v4, /device:TPU:0, one launch (start us, length us, event | category | flops | bytes accessed | tf_op | source)
XLA Modules:
  0.0 98.3 jit_solution(10617737470537366432)
XLA Ops:
  0.0 0.0 copy-start
  0.0 1.2 %copy-done = bf16[8,256,256]{2,1,0:T(8,128)(2,1)S(1)} copy-done((bf16[8,256,256]{2,1,0:T(8,128)(2,1)S(1)}, bf16[8,256,256]{2,1,0:T(8,128)(2,1)}, u32[]{:S(2)}) %copy-start) | copy-done | bytes 1048600
  1.2 0.0 copy-start.1
  1.2 1.2 %copy-done.1 = bf16[512,1024]{1,0:T(8,128)(2,1)S(1)} copy-done((bf16[512,1024]{1,0:T(8,128)(2,1)S(1)}, bf16[512,1024]{1,0:T(8,128)(2,1)}, u32[]{:S(2)}) %copy-start.1) | copy-done | bytes 1048600
  2.5 0.0 copy-start.2
  2.5 0.7 copy-done.2
  3.2 0.0 copy-start.3
  3.2 0.7 copy-done.3
  3.8 93.1 %shard_map.55 = f32[512,1024]{1,0:T(8,128)S(1)} custom-call(s32[3,8,8]{2,1,0:T(8,128)S(1)} %bitcast.3, s32[8,8]{1,0:T(8,128)S(1)} %copy-done.3, bf16[8,256,256]{2,1,0:T(8,128)(2,1)S(1)} %copy-done, bf16[2,256,1024]{2,1,0:T(8,128)(2,1)S(1)} %bitcast.2, bf16[4,1024,1024]{2,1,0:T(8,128)(2,1)} %b_hbm.1), custom_call_target="tpu_custom_call" | custom-call | tf_op jit(solution)/shard_map/pallas_call | solution.py:206
  97.0 1.3 %copy.7 = f32[512,1024]{1,0:T(8,128)} copy(f32[512,1024]{1,0:T(8,128)S(1)} %shard_map.55) | data formatting | bytes 4194304
Async XLA Ops:
  0.0 1.2 %copy-start = (bf16[8,256,256]{2,1,0:T(8,128)(2,1)S(1)}, bf16[8,256,256]{2,1,0:T(8,128)(2,1)}, u32[]{:S(2)}) copy-start(bf16[8,256,256]{2,1,0:T(8,128)(2,1)} %coupling_ref.1) | copy-start | bytes 3145732
  1.2 1.2 %copy-start.1 = (bf16[512,1024]{1,0:T(8,128)(2,1)S(1)}, bf16[512,1024]{1,0:T(8,128)(2,1)}, u32[]{:S(2)}) copy-start(bf16[512,1024]{1,0:T(8,128)(2,1)} %param.5) | copy-start | bytes 3145732
  2.5 0.7 copy-start.2
  3.2 0.7 copy-start.3
